TPU v7x, 32 devices: a whole 2x2x4 slice. The times are simulated.
32 devices in a mesh: dp: 16 (over z, y, x), tensor: 2 (over core).
Axes of the slice: x: 2, y: 2, z: 4, core: 2. Of those that a mesh axis runs over, the one named last changes fastest.
Arguments:
- acts: bfloat16 [1, 6144, 28672], P(None, 'dp', 'tensor'), may hold values from -6 to 6
- out_grads: bfloat16 [1, 6144, 8192], P(None, 'dp', 'tensor'), may hold values from -6 to 6
- proj_in: bfloat16 [1, 28672, 64], P(None, 'tensor'), may hold values from -0.03125 to 0.03125
- proj_out: bfloat16 [1, 8192, 64], P(None, 'tensor'), may hold values from -0.0625 to 0.0625
- doc_starts: int32 [64], P('dp'), may hold values from 0 to 191, as said below
- token_counts: int32 [16], P('dp'), may hold values from 192 to 384, as said below
- queries: float32 [256, 1, 4096], P('dp', None, 'tensor'), may hold values from -0.046875 to 0.046875
Outputs:
- scores: float32 [256, 64], P(None, 'dp')
- doc_grads: float32 [64, 1, 4096], P('dp', None, 'tensor')
Inputs may be any that keep to these rules, and one draw needn't show every extreme that they name: `doc_starts`: within each block of 4 entries the first is 0, the entries rise strictly, and the last is 191. `token_counts`: entry 0 equals 384.
All inputs are finite; a program needn't handle non-finite values.
Results may differ from a plain program's by a relative error of at most 0.0003.
Values sent between devices are 32-bit elements; how exact they have to be, the bound alone decides.
A program may use at most 64 MiB of HBM per device.

v0:
```python
import jax
import jax.numpy as jnp
from jax import lax
from jax.sharding import PartitionSpec as P


def document_products(member, left, right):
    spread = member[None, :, :, None] * left[:, :, None, :]
    grads = jnp.einsum("ltdr,lts->dlrs", spread, right, precision=lax.Precision.HIGHEST)
    return grads.reshape(grads.shape[0], grads.shape[1], grads.shape[2] * grads.shape[3])


def shards(acts, out_grads, proj_in, proj_out, doc_starts, token_counts, queries):
    layer_count = acts.shape[0]
    tok_rows = acts.shape[1]
    rank_size = proj_in.shape[2]
    docs_local = doc_starts.shape[0]
    left = jnp.stack([jnp.dot(acts[0], proj_in[0], preferred_element_type=jnp.float32)])
    right = jnp.stack([jnp.dot(out_grads[0], proj_out[0], preferred_element_type=jnp.float32)])
    positions = jnp.arange(tok_rows, dtype=jnp.int32)
    doc_index = jnp.sum((positions[:, None] >= doc_starts[None, :]).astype(jnp.int32), axis=1) - 1
    valid = positions < token_counts[0]
    member = (
        (doc_index[:, None] == jnp.arange(docs_local, dtype=jnp.int32)[None, :]) & valid[:, None]
    ).astype(jnp.float32)
    width = lax.axis_size("tensor")
    slot = lax.axis_index("tensor")
    share_width = rank_size * rank_size // width
    left, right = lax.psum((left, right), "tensor")
    full_grads = document_products(member, left, right)
    mine = lax.dynamic_slice_in_dim(full_grads, slot * share_width, share_width, 2)
    flat_grads = mine.reshape(docs_local, layer_count * share_width)
    piece = lax.all_gather(queries, "dp", axis=0, tiled=True)
    rows = piece.reshape(piece.shape[0], layer_count * share_width)
    partial_scores = jnp.dot(
        rows, flat_grads.T, precision=lax.Precision.HIGHEST, preferred_element_type=jnp.float32
    )
    scores = lax.psum(partial_scores, "tensor")
    return (scores, mine)


def solution(mesh):
    in_specs = (
        P(None, "dp", "tensor"),
        P(None, "dp", "tensor"),
        P(None, "tensor", None),
        P(None, "tensor", None),
        P("dp"),
        P("dp"),
        P("dp", None, "tensor"),
    )
    out_specs = (P(None, "dp"), P("dp", None, "tensor"))
    return jax.shard_map(shards, mesh=mesh, in_specs=in_specs, out_specs=out_specs, check_vma=False)
```

profile of v0, /device:TPU:0, one launch (start us, length us, event | category | flops | bytes accessed | tf_op | source)
XLA Modules:
  0.0 99.2 jit_solution(14235674293041148226)
XLA Ops:
  8.0 0.0 copy-start
  8.0 0.0 all-reduce.3.cloned.1.call-start
  8.1 0.0 copy-start.1
  8.1 8.9 %fusion = f32[384,64]{0,1:T(8,128)} fusion(bf16[1,384,14336]{2,1,0:T(8,128)(2,1)} %param.7, bf16[1,14336,64]{1,2,0:T(8,128)(2,1)} %param.9), kind=kOutput, calls=%fused_computation | convolution fusion | flops 704643072 | bytes 12943360 | tf_op jit(solution)/shard_map/dot_general | solution.py:18
  17.0 0.0 copy-done
  17.0 0.0 copy-done.1
  17.0 0.0 copy-start.2
  17.0 1.7 %fusion.2 = f32[384,64]{0,1:T(8,128)} fusion(bf16[1,384,4096]{2,1,0:T(8,128)(2,1)S(1)} %copy-done, bf16[1,4096,64]{1,2,0:T(8,128)(2,1)S(1)} %copy-done.1), kind=kOutput, calls=%fused_computation.2 | convolution fusion | flops 201326592 | bytes 3768320 | tf_op jit(solution)/shard_map/dot_general | solution.py:19
  18.7 0.0 all-reduce.3.cloned.1.call-update
  18.7 0.0 all-gather.2.cloned.1.call-start
  18.8 0.5 all-gather.2.cloned.1.call-update
  20.0 0.0 copy-done.2
  20.0 0.1 convert_reduce_fusion
  20.1 19.6 %all-reduce.3.cloned.1.call-done = (f32[384,64]{0,1:T(8,128)}, f32[384,64]{0,1:T(8,128)}) async-done(((f32[384,64]{0,1:T(8,128)}, f32[384,64]{0,1:T(8,128)}), (f32[384,64]{0,1:T(8,128)}, f32[384,64]{0,1:T(8,128)})) %all-reduce.3.cloned.1.call-update) | async-done | bytes 196624 | tf_op jit(solution)/shard_map/psum | solution.py:29
  39.7 1.8 %convolution_bitcast_fusion = f32[4,1,64,64]{2,3,0,1:T(8,128)S(1)} fusion(f32[384,64]{0,1:T(8,128)} %get-tuple-element.8, f32[384,4]{0,1:T(4,128)S(1)} %fusion.18, f32[384,64]{0,1:T(8,128)} %get-tuple-element.9), kind=kOutput, calls=%fused_computation.8 | convolution fusion | flops 75595776 | bytes 268288 | tf_op jit(solution)/shard_map/ltdr,lts->dlrs/dot_general | solution.py:9
  41.5 0.1 copy.13
  41.6 0.1 reshape.72
  41.8 0.6 copy.14
  42.4 42.8 %all-gather.2.cloned.1.call-done = f32[256,1,2048]{2,1,0:T(1,128)} async-done(((f32[16,1,2048]{2,1,0:T(1,128)}), f32[256,1,2048]{2,1,0:T(1,128)}) %all-gather.2.cloned.1.call-update) | async-done | bytes 2097168 | tf_op jit(solution)/shard_map/all_gather | solution.py:33
  85.2 3.5 %fusion.8 = f32[256,4]{0,1:T(4,128)S(1)} fusion(f32[256,1,2048]{2,1,0:T(1,128)} %all-gather.2.cloned.1.call-done, f32[4,1,2048]{2,0,1:T(4,128)S(1)} %constant_dynamic-slice_fusion), kind=kOutput, calls=%fused_computation.9 | convolution fusion | flops 25165824 | bytes 2134016 | tf_op jit(solution)/shard_map/dot_general | solution.py:35
  88.7 3.1 %psum.23 = f32[256,4]{0,1:T(4,128)} all-reduce(f32[256,4]{0,1:T(4,128)S(1)} %fusion.8), channel_id=1, replica_groups=mesh['dp'=16,'tensor'=2] {'tensor'}, use_global_device_ids=true, to_apply=%region_3.0 | all-reduce | flops 1024 | bytes 8192 | tf_op jit(solution)/shard_map/psum | solution.py:38
  (4 shorter events, 0.0 us)
Async XLA Ops:
  8.0 9.0 %copy-start = (bf16[1,384,4096]{2,1,0:T(8,128)(2,1)S(1)}, bf16[1,384,4096]{2,1,0:T(8,128)(2,1)}, u32[]{:S(2)}) copy-start(bf16[1,384,4096]{2,1,0:T(8,128)(2,1)} %param.8) | copy-start | bytes 9437188
  8.0 31.7 %all-reduce.3.cloned.1.call-start = ((), (), s32[]{:S(2)}) async-start(), calls=%async_computation.1 | async-start | bytes 393216 | tf_op jit(solution)/shard_map/psum | solution.py:29
  8.1 8.9 %copy-start.1 = (bf16[1,4096,64]{1,2,0:T(8,128)(2,1)S(1)}, bf16[1,4096,64]{1,2,0:T(8,128)(2,1)}, u32[]{:S(2)}) copy-start(bf16[1,4096,64]{1,2,0:T(8,128)(2,1)} %param.10) | copy-start | bytes 1572868
  17.0 3.0 %copy-start.2 = (s32[4]{0:T(128)S(1)}, s32[4]{0:T(128)}, u32[]{:S(2)}) copy-start(s32[4]{0:T(128)} %param.11) | copy-start | bytes 52
  18.7 66.5 %all-gather.2.cloned.1.call-start = ((), (), s32[]{:S(2)}) async-start(), calls=%async_computation | async-start | bytes 2228224 | tf_op jit(solution)/shard_map/all_gather | solution.py:33
Sparse Core Ops, SparseCore 0:
  18.8 20.8 all-reduce.2
Sparse Core Ops, SparseCore 1:
  22.0 63.2 all-gather.1
where the time goes:
time: 99.4 us; the launch traced here: 99.2 us
  waiting for transfers between devices  63 us (63%)
  between operations  16.2 us (16%)
  matrix products  15.9 us (16%)
  blocking collectives  3.05 us (3%)
    all_gather x1, waiting for transfers between devices, shards(): piece = lax.all_gather(queries, 'dp', axis=0, tiled=True)  42.8 us
    psum x1, waiting for transfers between devices, shards(): left, right = lax.psum((left, right), 'tensor')  19.6 us
    dot_general x1, matrix products, shards(): jnp.dot(acts[0], proj_in[0], preferred_element_type=jnp.float32)  8.88 us
    dot_general x1, matrix products, shards(): jnp.dot(rows, flat_grads.T, precision=lax.Precision.HIGHEST, preferred_el...  3.52 us
    psum x1, blocking collectives, shards(): scores = lax.psum(partial_scores, 'tensor')  3.05 us
  transfers between devices with their start and end apart: 2, of which 2 were waited for; matrix products, arithmetic and copies ran while one was open for 3% of the time, Pallas kernels for 0%

commit v1 on v0

--- a/solution.py
+++ b/solution.py
@@ -1,7 +1,26 @@
+import functools
 import jax
 import jax.numpy as jnp
 from jax import lax
 from jax.sharding import PartitionSpec as P
+
+
+def enter_the_spot(work_x, mesh_ax):
+    axis_total = lax.axis_size(mesh_ax)
+    steps_seen = list(map(lambda to_i: (to_i, (to_i + 1) % axis_total), range(axis_total)))
+
+    def tiles_process(view_out):
+        if len(view_out) == axis_total:
+            return view_out
+        oldest = tiles_process([lax.ppermute(view_out[0], mesh_ax, steps_seen), *view_out])
+        return oldest
+
+    x_new = jnp.concatenate(tiles_process([work_x]), axis=0)
+    z_new = jnp.roll(x_new, (lax.axis_index(mesh_ax) + 1) * work_x.shape[0], 0)
+    return z_new
+
+
+fill_chains = functools.partial(enter_the_spot, mesh_ax="dp")
 
 
 def document_products(member, left, right):
@@ -30,7 +49,7 @@
     full_grads = document_products(member, left, right)
     mine = lax.dynamic_slice_in_dim(full_grads, slot * share_width, share_width, 2)
     flat_grads = mine.reshape(docs_local, layer_count * share_width)
-    piece = lax.all_gather(queries, "dp", axis=0, tiled=True)
+    piece = fill_chains(queries)
     rows = piece.reshape(piece.shape[0], layer_count * share_width)
     partial_scores = jnp.dot(
         rows, flat_grads.T, precision=lax.Precision.HIGHEST, preferred_element_type=jnp.float32

time: 99.4 us -> 176 us (1.77)
  waiting for transfers between devices: 63 us -> 112 us
  local copies, waits for them, and re-layouts: 0.88 us -> 25.2 us
  starting transfers between devices: 0.08 us -> 4.97 us
    ppermute x0 -> x15, waiting for transfers between devices: none -> 108 us  [tiles_process(): lax.ppermute(view_out[0], mesh_ax, steps_seen)]
    all_gather x1 -> x0, waiting for transfers between devices: 42.8 us -> none  [shards(): piece = lax.all_gather(queries, 'dp', axis=0, tiled=True)]
    unnamed x7 -> x72, local copies, waits for them, and re-layouts: 0.67 us -> 19.7 us
    psum x1, waiting for transfers between devices: 19.6 us -> 4.16 us  [shards(): left, right = lax.psum((left, right), 'tensor')]
    ppermute x0 -> x15, starting transfers between devices: none -> 4.94 us  [tiles_process(): lax.ppermute(view_out[0], mesh_ax, steps_seen)]
  transfers between devices with their start and end apart: 2 -> 16, of which waited for: 2 -> 14; matrix products, arithmetic and copies ran while one was open for 3% -> 10% of each run, Pallas kernels for 0% -> 0%
where the time goes in v1:
time: 176 us
  waiting for transfers between devices  112 us (64%)
  local copies, waits for them, and re-layouts  25.2 us (14%)
  matrix products  15.1 us (9%)
  between operations  15.1 us (9%)
  starting transfers between devices  4.97 us (3%)
  blocking collectives  3.05 us (2%)
    ppermute x15, waiting for transfers between devices, tiles_process(): lax.ppermute(view_out[0], mesh_ax, steps_seen)  108 us
    unnamed x72, local copies, waits for them, and re-layouts  19.7 us
    dot_general x1, matrix products, shards(): jnp.dot(acts[0], proj_in[0], preferred_element_type=jnp.float32)  8.78 us
    ppermute x15, starting transfers between devices, tiles_process(): lax.ppermute(view_out[0], mesh_ax, steps_seen)  4.94 us
    psum x1, waiting for transfers between devices, shards(): left, right = lax.psum((left, right), 'tensor')  4.16 us
  transfers between devices with their start and end apart: 16, of which 14 were waited for; matrix products, arithmetic and copies ran while one was open for 10% of the time, Pallas kernels for 0%

profile of v1, /device:TPU:0, one launch (start us, length us, event | category | flops | bytes accessed | tf_op | source)
XLA Modules:
  0.0 175.6 jit_solution(6254717181464085074)
XLA Ops:
  7.2 3.0 %collective-permute-start = (f32[16,1,2048]{2,1,0:T(1,128)}, f32[16,1,2048]{2,1,0:T(1,128)S(1)}, u32[]{:S(2)}, u32[]{:S(2)}) collective-permute-start(f32[16,1,2048]{2,1,0:T(1,128)} %param.13), channel_id=1, source_target_pairs={{0,2},{2,4},{4,6},{6,8},{8,10},{10,12},{12,14},{14,16},{16,18},{18... | collective-permute-start | bytes 393224 | tf_op jit(solution)/shard_map/ppermute | solution.py:15
  10.3 7.7 %collective-permute-done = f32[16,1,2048]{2,1,0:T(1,128)S(1)} collective-permute-done((f32[16,1,2048]{2,1,0:T(1,128)}, f32[16,1,2048]{2,1,0:T(1,128)S(1)}, u32[]{:S(2)}, u32[]{:S(2)}) %collective-permute-start) | collective-permute-done | bytes 131104 | tf_op jit(solution)/shard_map/ppermute | solution.py:15
  18.0 8.6 %collective-permute-done.1 = f32[16,1,2048]{2,1,0:T(1,128)S(1)} collective-permute-done((f32[16,1,2048]{2,1,0:T(1,128)S(1)}, f32[16,1,2048]{2,1,0:T(1,128)S(1)}, u32[]{:S(2)}, u32[]{:S(2)}) %collective-permute-start.1) | collective-permute-done | bytes 131104 | tf_op jit(solution)/shard_map/ppermute | solution.py:15
  26.5 8.6 %collective-permute-done.2 = f32[16,1,2048]{2,1,0:T(1,128)S(1)} collective-permute-done((f32[16,1,2048]{2,1,0:T(1,128)S(1)}, f32[16,1,2048]{2,1,0:T(1,128)S(1)}, u32[]{:S(2)}, u32[]{:S(2)}) %collective-permute-start.2) | collective-permute-done | bytes 131104 | tf_op jit(solution)/shard_map/ppermute | solution.py:15
  35.1 8.6 %collective-permute-done.3 = f32[16,1,2048]{2,1,0:T(1,128)S(1)} collective-permute-done((f32[16,1,2048]{2,1,0:T(1,128)S(1)}, f32[16,1,2048]{2,1,0:T(1,128)S(1)}, u32[]{:S(2)}, u32[]{:S(2)}) %collective-permute-start.3) | collective-permute-done | bytes 131104 | tf_op jit(solution)/shard_map/ppermute | solution.py:15
  44.3 8.6 %collective-permute-done.4 = f32[16,1,2048]{2,1,0:T(1,128)S(1)} collective-permute-done((f32[16,1,2048]{2,1,0:T(1,128)S(1)}, f32[16,1,2048]{2,1,0:T(1,128)S(1)}, u32[]{:S(2)}, u32[]{:S(2)}) %collective-permute-start.4) | collective-permute-done | bytes 131104 | tf_op jit(solution)/shard_map/ppermute | solution.py:15
  53.5 8.6 %collective-permute-done.5 = f32[16,1,2048]{2,1,0:T(1,128)S(1)} collective-permute-done((f32[16,1,2048]{2,1,0:T(1,128)S(1)}, f32[16,1,2048]{2,1,0:T(1,128)S(1)}, u32[]{:S(2)}, u32[]{:S(2)}) %collective-permute-start.5) | collective-permute-done | bytes 131104 | tf_op jit(solution)/shard_map/ppermute | solution.py:15
  62.7 9.4 %collective-permute-done.6 = f32[16,1,2048]{2,1,0:T(1,128)S(1)} collective-permute-done((f32[16,1,2048]{2,1,0:T(1,128)S(1)}, f32[16,1,2048]{2,1,0:T(1,128)S(1)}, u32[]{:S(2)}, u32[]{:S(2)}) %collective-permute-start.6) | collective-permute-done | bytes 131104 | tf_op jit(solution)/shard_map/ppermute | solution.py:15
  72.7 9.4 %collective-permute-done.7 = f32[16,1,2048]{2,1,0:T(1,128)S(1)} collective-permute-done((f32[16,1,2048]{2,1,0:T(1,128)S(1)}, f32[16,1,2048]{2,1,0:T(1,128)S(1)}, u32[]{:S(2)}, u32[]{:S(2)}) %collective-permute-start.7) | collective-permute-done | bytes 131104 | tf_op jit(solution)/shard_map/ppermute | solution.py:15
  82.8 8.6 %collective-permute-done.8 = f32[16,1,2048]{2,1,0:T(1,128)S(1)} collective-permute-done((f32[16,1,2048]{2,1,0:T(1,128)S(1)}, f32[16,1,2048]{2,1,0:T(1,128)S(1)}, u32[]{:S(2)}, u32[]{:S(2)}) %collective-permute-start.8) | collective-permute-done | bytes 131104 | tf_op jit(solution)/shard_map/ppermute | solution.py:15
  92.0 8.6 %collective-permute-done.9 = f32[16,1,2048]{2,1,0:T(1,128)S(1)} collective-permute-done((f32[16,1,2048]{2,1,0:T(1,128)S(1)}, f32[16,1,2048]{2,1,0:T(1,128)S(1)}, u32[]{:S(2)}, u32[]{:S(2)}) %collective-permute-start.9) | collective-permute-done | bytes 131104 | tf_op jit(solution)/shard_map/ppermute | solution.py:15
  100.6 8.8 %fusion = f32[384,64]{0,1:T(8,128)} fusion(bf16[1,384,14336]{2,1,0:T(8,128)(2,1)} %param.7, bf16[1,14336,64]{1,2,0:T(8,128)(2,1)} %param.9), kind=kOutput, calls=%fused_computation | convolution fusion | flops 704643072 | bytes 12943360 | tf_op jit(solution)/shard_map/dot_general | solution.py:37
  109.5 1.7 fusion.2
  111.3 7.0 %collective-permute-done.11 = f32[16,1,2048]{2,1,0:T(1,128)} collective-permute-done((f32[16,1,2048]{2,1,0:T(1,128)}, f32[16,1,2048]{2,1,0:T(1,128)}, u32[]{:S(2)}, u32[]{:S(2)}) %collective-permute-start.11) | collective-permute-done | bytes 131104 | tf_op jit(solution)/shard_map/ppermute | solution.py:15
  119.0 8.2 %collective-permute-done.12 = f32[16,1,2048]{2,1,0:T(1,128)} collective-permute-done((f32[16,1,2048]{2,1,0:T(1,128)}, f32[16,1,2048]{2,1,0:T(1,128)}, u32[]{:S(2)}, u32[]{:S(2)}) %collective-permute-start.12) | collective-permute-done | bytes 131104 | tf_op jit(solution)/shard_map/ppermute | solution.py:15
  127.3 4.2 %all-reduce.3.cloned.1.call-done = (f32[384,64]{0,1:T(8,128)}, f32[384,64]{0,1:T(8,128)}) async-done(((f32[384,64]{0,1:T(8,128)}, f32[384,64]{0,1:T(8,128)}), (f32[384,64]{0,1:T(8,128)}, f32[384,64]{0,1:T(8,128)})) %all-reduce.3.cloned.1.call-update) | async-done | bytes 196624 | tf_op jit(solution)/shard_map/psum | solution.py:48
  131.4 2.5 %convolution_bitcast_fusion = f32[4,1,64,64]{2,3,0,1:T(8,128)} fusion(f32[384,64]{0,1:T(8,128)} %get-tuple-element.6, f32[384,4]{0,1:T(4,128)S(1)} %fusion.15, f32[384,64]{0,1:T(8,128)} %get-tuple-element.7), kind=kOutput, calls=%fused_computation.8 | convolution fusion | flops 75595776 | bytes 268288 | tf_op jit(solution)/shard_map/ltdr,lts->dlrs/dot_general | solution.py:28
  133.9 1.7 copy.11
  135.5 1.6 reshape.73
  137.2 1.8 %collective-permute-start.14 = (f32[16,1,2048]{2,1,0:T(1,128)}, f32[16,1,2048]{2,1,0:T(1,128)S(1)}, u32[]{:S(2)}, u32[]{:S(2)}) collective-permute-start(f32[16,1,2048]{2,1,0:T(1,128)} %collective-permute-done.13), channel_id=1, source_target_pairs={{0,2},{2,4},{4,6},{6,8},{8,10},{10,12},{12,14},{14,16},{16,18},{18... | collective-permute-start | bytes 393224 | tf_op jit(solution)/shard_map/ppermute | solution.py:15
  140.5 6.4 %collective-permute-done.14 = f32[16,1,2048]{2,1,0:T(1,128)S(1)} collective-permute-done((f32[16,1,2048]{2,1,0:T(1,128)}, f32[16,1,2048]{2,1,0:T(1,128)S(1)}, u32[]{:S(2)}, u32[]{:S(2)}) %collective-permute-start.14) | collective-permute-done | bytes 131104 | tf_op jit(solution)/shard_map/ppermute | solution.py:15
  146.9 0.9 constant_dynamic-update-slice_fusion.30
  147.8 0.9 constant_dynamic-update-slice_fusion.29
  148.7 0.9 constant_dynamic-update-slice_fusion.28
  149.6 0.9 constant_dynamic-update-slice_fusion.27
  150.6 0.9 constant_dynamic-update-slice_fusion.26
  151.5 0.9 constant_dynamic-update-slice_fusion.25
  153.4 0.9 constant_dynamic-update-slice_fusion.23
  154.3 0.9 constant_dynamic-update-slice_fusion.22
  162.2 1.4 constant_dynamic-slice_fusion.1
  163.7 2.1 %fusion.4 = f32[256,4]{0,1:T(4,128)S(1)} fusion(f32[256,1,2048]{2,1,0:T(1,128)S(1)} %constant_dynamic-slice_fusion.1, f32[4,1,2048]{2,0,1:T(4,128)S(1)} %constant_dynamic-slice_fusion), kind=kOutput, calls=%fused_computation.4 | convolution fusion | flops 25165824 | bytes 2134016 | tf_op jit(solution)/shard_map/dot_general | solution.py:54
  165.7 3.0 %psum.23 = f32[256,4]{0,1:T(4,128)} all-reduce(f32[256,4]{0,1:T(4,128)S(1)} %fusion.4), channel_id=1, replica_groups=mesh['dp'=16,'tensor'=2] {'tensor'}, use_global_device_ids=true, to_apply=%region_3.4 | all-reduce | flops 1024 | bytes 8192 | tf_op jit(solution)/shard_map/psum | solution.py:57
  (87 shorter events, 13.3 us)
Async XLA Ops:
  7.2 102.3 %copy-start = (bf16[1,384,4096]{2,1,0:T(8,128)(2,1)S(1)}, bf16[1,384,4096]{2,1,0:T(8,128)(2,1)}, u32[]{:S(2)}) copy-start(bf16[1,384,4096]{2,1,0:T(8,128)(2,1)} %param.8) | copy-start | bytes 9437188
  7.2 124.2 %all-reduce.3.cloned.1.call-start = ((), (), s32[]{:S(2)}) async-start(), calls=%async_computation | async-start | bytes 393216 | tf_op jit(solution)/shard_map/psum | solution.py:48
  7.2 102.3 %copy-start.1 = (bf16[1,4096,64]{1,2,0:T(8,128)(2,1)S(1)}, bf16[1,4096,64]{1,2,0:T(8,128)(2,1)}, u32[]{:S(2)}) copy-start(bf16[1,4096,64]{1,2,0:T(8,128)(2,1)} %param.10) | copy-start | bytes 1572868
  7.2 10.7 %collective-permute-start = (f32[16,1,2048]{2,1,0:T(1,128)}, f32[16,1,2048]{2,1,0:T(1,128)S(1)}, u32[]{:S(2)}, u32[]{:S(2)}) collective-permute-start(f32[16,1,2048]{2,1,0:T(1,128)} %param.13), channel_id=1, source_target_pairs={{0,2},{2,4},{4,6},{6,8},{8,10},{10,12},{12,14},{14,16},{16,18},{18... | collective-permute-start | bytes 393224 | tf_op jit(solution)/shard_map/ppermute | solution.py:15
  18.0 8.6 %collective-permute-start.1 = (f32[16,1,2048]{2,1,0:T(1,128)S(1)}, f32[16,1,2048]{2,1,0:T(1,128)S(1)}, u32[]{:S(2)}, u32[]{:S(2)}) collective-permute-start(f32[16,1,2048]{2,1,0:T(1,128)S(1)} %collective-permute-done), channel_id=1, source_target_pairs={{0,2},{2,4},{4,6},{6,8},{8,10},{10,12},{12,14},{14,16},{16,18},{18... | collective-permute-start | bytes 393224 | tf_op jit(solution)/shard_map/ppermute | solution.py:15
  26.5 8.6 %collective-permute-start.2 = (f32[16,1,2048]{2,1,0:T(1,128)S(1)}, f32[16,1,2048]{2,1,0:T(1,128)S(1)}, u32[]{:S(2)}, u32[]{:S(2)}) collective-permute-start(f32[16,1,2048]{2,1,0:T(1,128)S(1)} %collective-permute-done.1), channel_id=1, source_target_pairs={{0,2},{2,4},{4,6},{6,8},{8,10},{10,12},{12,14},{14,16},{16,18},{18... | collective-permute-start | bytes 393224 | tf_op jit(solution)/shard_map/ppermute | solution.py:15
  35.1 65.5 %copy-start.3 = (f32[16,1,2048]{2,1,0:T(1,128)}, f32[16,1,2048]{2,1,0:T(1,128)S(1)}, u32[]{:S(2)}) copy-start(f32[16,1,2048]{2,1,0:T(1,128)S(1)} %collective-permute-done.2) | copy-start | bytes 393220
  35.1 8.6 %collective-permute-start.3 = (f32[16,1,2048]{2,1,0:T(1,128)S(1)}, f32[16,1,2048]{2,1,0:T(1,128)S(1)}, u32[]{:S(2)}, u32[]{:S(2)}) collective-permute-start(f32[16,1,2048]{2,1,0:T(1,128)S(1)} %collective-permute-done.2), channel_id=1, source_target_pairs={{0,2},{2,4},{4,6},{6,8},{8,10},{10,12},{12,14},{14,16},{16,18},{18... | collective-permute-start | bytes 393224 | tf_op jit(solution)/shard_map/ppermute | solution.py:15
  44.3 8.6 %collective-permute-start.4 = (f32[16,1,2048]{2,1,0:T(1,128)S(1)}, f32[16,1,2048]{2,1,0:T(1,128)S(1)}, u32[]{:S(2)}, u32[]{:S(2)}) collective-permute-start(f32[16,1,2048]{2,1,0:T(1,128)S(1)} %collective-permute-done.3), channel_id=1, source_target_pairs={{0,2},{2,4},{4,6},{6,8},{8,10},{10,12},{12,14},{14,16},{16,18},{18... | collective-permute-start | bytes 393224 | tf_op jit(solution)/shard_map/ppermute | solution.py:15
  53.5 8.6 %collective-permute-start.5 = (f32[16,1,2048]{2,1,0:T(1,128)S(1)}, f32[16,1,2048]{2,1,0:T(1,128)S(1)}, u32[]{:S(2)}, u32[]{:S(2)}) collective-permute-start(f32[16,1,2048]{2,1,0:T(1,128)S(1)} %collective-permute-done.4), channel_id=1, source_target_pairs={{0,2},{2,4},{4,6},{6,8},{8,10},{10,12},{12,14},{14,16},{16,18},{18... | collective-permute-start | bytes 393224 | tf_op jit(solution)/shard_map/ppermute | solution.py:15
  62.1 0.7 copy-start.9
  62.7 9.4 %collective-permute-start.6 = (f32[16,1,2048]{2,1,0:T(1,128)S(1)}, f32[16,1,2048]{2,1,0:T(1,128)S(1)}, u32[]{:S(2)}, u32[]{:S(2)}) collective-permute-start(f32[16,1,2048]{2,1,0:T(1,128)S(1)} %collective-permute-done.5), channel_id=1, source_target_pairs={{0,2},{2,4},{4,6},{6,8},{8,10},{10,12},{12,14},{14,16},{16,18},{18... | collective-permute-start | bytes 393224 | tf_op jit(solution)/shard_map/ppermute | solution.py:15
  72.7 9.4 %collective-permute-start.7 = (f32[16,1,2048]{2,1,0:T(1,128)S(1)}, f32[16,1,2048]{2,1,0:T(1,128)S(1)}, u32[]{:S(2)}, u32[]{:S(2)}) collective-permute-start(f32[16,1,2048]{2,1,0:T(1,128)S(1)} %collective-permute-done.6), channel_id=1, source_target_pairs={{0,2},{2,4},{4,6},{6,8},{8,10},{10,12},{12,14},{14,16},{16,18},{18... | collective-permute-start | bytes 393224 | tf_op jit(solution)/shard_map/ppermute | solution.py:15
  82.2 0.7 copy-start.13
  82.8 8.6 %collective-permute-start.8 = (f32[16,1,2048]{2,1,0:T(1,128)S(1)}, f32[16,1,2048]{2,1,0:T(1,128)S(1)}, u32[]{:S(2)}, u32[]{:S(2)}) collective-permute-start(f32[16,1,2048]{2,1,0:T(1,128)S(1)} %collective-permute-done.7), channel_id=1, source_target_pairs={{0,2},{2,4},{4,6},{6,8},{8,10},{10,12},{12,14},{14,16},{16,18},{18... | collective-permute-start | bytes 393224 | tf_op jit(solution)/shard_map/ppermute | solution.py:15
  92.0 8.6 %collective-permute-start.9 = (f32[16,1,2048]{2,1,0:T(1,128)S(1)}, f32[16,1,2048]{2,1,0:T(1,128)S(1)}, u32[]{:S(2)}, u32[]{:S(2)}) collective-permute-start(f32[16,1,2048]{2,1,0:T(1,128)S(1)} %collective-permute-done.8), channel_id=1, source_target_pairs={{0,2},{2,4},{4,6},{6,8},{8,10},{10,12},{12,14},{14,16},{16,18},{18... | collective-permute-start | bytes 393224 | tf_op jit(solution)/shard_map/ppermute | solution.py:15
  100.6 8.8 %copy-start.17 = (f32[16,1,2048]{2,1,0:T(1,128)}, f32[16,1,2048]{2,1,0:T(1,128)S(1)}, u32[]{:S(2)}) copy-start(f32[16,1,2048]{2,1,0:T(1,128)S(1)} %collective-permute-done.9) | copy-start | bytes 393220
  100.6 8.8 %collective-permute-start.10 = (f32[16,1,2048]{2,1,0:T(1,128)S(1)}, f32[16,1,2048]{2,1,0:T(1,128)}, u32[]{:S(2)}, u32[]{:S(2)}) collective-permute-start(f32[16,1,2048]{2,1,0:T(1,128)S(1)} %collective-permute-done.9), channel_id=1, source_target_pairs={{0,2},{2,4},{4,6},{6,8},{8,10},{10,12},{12,14},{14,16},{16,18},{18... | collective-permute-start | bytes 393224 | tf_op jit(solution)/shard_map/ppermute | solution.py:15
  109.4 1.8 %copy-start.19 = (s32[4]{0:T(128)S(1)}, s32[4]{0:T(128)}, u32[]{:S(2)}) copy-start(s32[4]{0:T(128)} %param.11) | copy-start | bytes 52
  109.4 48.6 %copy-start.2 = (f32[16,1,2048]{2,1,0:T(1,128)S(1)}, f32[16,1,2048]{2,1,0:T(1,128)}, u32[]{:S(2)}) copy-start(f32[16,1,2048]{2,1,0:T(1,128)} %param.13) | copy-start | bytes 393220
  109.4 8.9 %collective-permute-start.11 = (f32[16,1,2048]{2,1,0:T(1,128)}, f32[16,1,2048]{2,1,0:T(1,128)}, u32[]{:S(2)}, u32[]{:S(2)}) collective-permute-start(f32[16,1,2048]{2,1,0:T(1,128)} %collective-permute-done.10), channel_id=1, source_target_pairs={{0,2},{2,4},{4,6},{6,8},{8,10},{10,12},{12,14},{14,16},{16,18},{18... | collective-permute-start | bytes 393224 | tf_op jit(solution)/shard_map/ppermute | solution.py:15
  118.3 8.9 %collective-permute-start.12 = (f32[16,1,2048]{2,1,0:T(1,128)}, f32[16,1,2048]{2,1,0:T(1,128)}, u32[]{:S(2)}, u32[]{:S(2)}) collective-permute-start(f32[16,1,2048]{2,1,0:T(1,128)} %collective-permute-done.11), channel_id=1, source_target_pairs={{0,2},{2,4},{4,6},{6,8},{8,10},{10,12},{12,14},{14,16},{16,18},{18... | collective-permute-start | bytes 393224 | tf_op jit(solution)/shard_map/ppermute | solution.py:15
  127.2 10.0 %collective-permute-start.13 = (f32[16,1,2048]{2,1,0:T(1,128)}, f32[16,1,2048]{2,1,0:T(1,128)}, u32[]{:S(2)}, u32[]{:S(2)}) collective-permute-start(f32[16,1,2048]{2,1,0:T(1,128)} %collective-permute-done.12), channel_id=1, source_target_pairs={{0,2},{2,4},{4,6},{6,8},{8,10},{10,12},{12,14},{14,16},{16,18},{18... | collective-permute-start | bytes 393224 | tf_op jit(solution)/shard_map/ppermute | solution.py:15
  137.2 24.7 %copy-start.18 = (f32[16,1,2048]{2,1,0:T(1,128)S(1)}, f32[16,1,2048]{2,1,0:T(1,128)}, u32[]{:S(2)}) copy-start(f32[16,1,2048]{2,1,0:T(1,128)} %copy-done.17) | copy-start | bytes 393220
  137.2 24.7 %copy-start.16 = (f32[16,1,2048]{2,1,0:T(1,128)S(1)}, f32[16,1,2048]{2,1,0:T(1,128)}, u32[]{:S(2)}) copy-start(f32[16,1,2048]{2,1,0:T(1,128)} %copy-done.15) | copy-start | bytes 393220
  137.2 24.7 %copy-start.14 = (f32[16,1,2048]{2,1,0:T(1,128)S(1)}, f32[16,1,2048]{2,1,0:T(1,128)}, u32[]{:S(2)}) copy-start(f32[16,1,2048]{2,1,0:T(1,128)} %copy-done.13) | copy-start | bytes 393220
  137.2 24.8 %copy-start.12 = (f32[16,1,2048]{2,1,0:T(1,128)S(1)}, f32[16,1,2048]{2,1,0:T(1,128)}, u32[]{:S(2)}) copy-start(f32[16,1,2048]{2,1,0:T(1,128)} %copy-done.11) | copy-start | bytes 393220
  137.2 24.8 %copy-start.10 = (f32[16,1,2048]{2,1,0:T(1,128)S(1)}, f32[16,1,2048]{2,1,0:T(1,128)}, u32[]{:S(2)}) copy-start(f32[16,1,2048]{2,1,0:T(1,128)} %copy-done.9) | copy-start | bytes 393220
  137.2 24.8 %copy-start.8 = (f32[16,1,2048]{2,1,0:T(1,128)S(1)}, f32[16,1,2048]{2,1,0:T(1,128)}, u32[]{:S(2)}) copy-start(f32[16,1,2048]{2,1,0:T(1,128)} %copy-done.7) | copy-start | bytes 393220
  137.2 24.8 %copy-start.6 = (f32[16,1,2048]{2,1,0:T(1,128)S(1)}, f32[16,1,2048]{2,1,0:T(1,128)}, u32[]{:S(2)}) copy-start(f32[16,1,2048]{2,1,0:T(1,128)} %copy-done.5) | copy-start | bytes 393220
  137.2 24.9 %copy-start.4 = (f32[16,1,2048]{2,1,0:T(1,128)S(1)}, f32[16,1,2048]{2,1,0:T(1,128)}, u32[]{:S(2)}) copy-start(f32[16,1,2048]{2,1,0:T(1,128)} %copy-done.3) | copy-start | bytes 393220
  137.2 9.6 %collective-permute-start.14 = (f32[16,1,2048]{2,1,0:T(1,128)}, f32[16,1,2048]{2,1,0:T(1,128)S(1)}, u32[]{:S(2)}, u32[]{:S(2)}) collective-permute-start(f32[16,1,2048]{2,1,0:T(1,128)} %collective-permute-done.13), channel_id=1, source_target_pairs={{0,2},{2,4},{4,6},{6,8},{8,10},{10,12},{12,14},{14,16},{16,18},{18... | collective-permute-start | bytes 393224 | tf_op jit(solution)/shard_map/ppermute | solution.py:15
  (4 other events, 2.6 us)
Sparse Core Ops, SparseCore 0:
  111.4 20.0 all-reduce.2
